TPU v7x, 32 devices: a whole 2x2x4 slice. The times are simulated.
32 devices in a mesh: groups: 2 (over x), gy: 16 (over z, y, core).
Axes of the slice: x: 2, y: 2, z: 4, core: 2. Of those that a mesh axis runs over, the one named last changes fastest.
Arguments:
- observed: float32 [2048, 16, 256], P(('groups', 'gy')), parts along dimension 0, may hold values from -6 to 6
- tf_table: float32 [16], replicated, may hold values from 0.2 to 2
- tilt_index: int32 [513, 129], replicated, may hold values from 0 to 15
- wedge: int32 [513, 129], replicated, may hold values 0 or 1
Outputs:
- restored: float32 [2048, 16, 256], P(('groups', 'gy')), parts along dimension 0
There are 2 independent parts, one for each index of `groups`. A program takes and returns all parts, laid end to end along the dimension named above; an argument that names none is the same for every part. Nothing has to cross between parts.
All inputs are finite; a program needn't handle non-finite values.
Results may differ from a plain program's by a relative error of at most 0.00011.
Values sent between devices are 32-bit elements; how exact they have to be, the bound alone decides.
A program may use at most 64 MiB of HBM per device.

v0:
```python
import math
import jax
import jax.numpy as jnp
from jax import lax
from jax.sharding import PartitionSpec as P

NX = 1024
OUTER = 2
PASSES = 2
step_dual = 0.14
step_primal = 0.14
huber_eps = 0.05
bound_dual = 0.5
highest = lax.Precision.HIGHEST


def extended(value, sides, width):
    for axis, dim in sides:
        devices, length = (lax.axis_size(axis), value.shape[dim])
        up = [(i, (i + 1) % devices) for i in range(devices - 1)]
        down = [(j, i) for i, j in up]
        last = lax.slice_in_dim(value, length - width, length, axis=dim)
        initial = lax.slice_in_dim(value, 0, width, axis=dim)
        before = lax.ppermute(last, axis, up)
        after = lax.ppermute(initial, axis, down)
        value = jnp.concatenate([before, value, after], axis=dim)
    return value


def curvature(field, axis):
    widths = [(0, 0), (0, 0), (0, 0)]
    widths[axis] = (1, 1)
    padded = jnp.pad(field, widths)
    upper = lax.slice_in_dim(padded, 2, padded.shape[axis], axis=axis)
    lower = lax.slice_in_dim(padded, 0, padded.shape[axis] - 2, axis=axis)
    return upper + lower - 2.0 * field


def rim_curvature(padded, field, axis):
    upper = lax.slice_in_dim(padded, 2, padded.shape[axis], axis=axis)
    lower = lax.slice_in_dim(padded, 0, padded.shape[axis] - 2, axis=axis)
    return upper + lower - 2.0 * field


def denoise(target, duals, sharded, primal_rim, dual_rim):
    field = target
    lead = target
    for sweep in range(PASSES):
        padded = primal_rim(lead)
        raised = []
        for axis in range(3):
            if axis == sharded:
                bend = rim_curvature(padded, lead, axis)
            else:
                bend = curvature(lead, axis)
            raised.append(
                (duals[axis] + step_dual * bend) / (1.0 + step_dual * huber_eps / bound_dual)
            )
        total = raised[0] * raised[0] + raised[1] * raised[1] + raised[2] * raised[2]
        shrink = jnp.sqrt(jnp.maximum(1.0, total / (bound_dual * bound_dual)))
        duals = (raised[0] / shrink, raised[1] / shrink, raised[2] / shrink)
        padded_dual = dual_rim(duals[sharded])
        adjoint = jnp.zeros_like(field)
        for axis in range(3):
            if axis == sharded:
                adjoint = rim_curvature(padded_dual, duals[axis], axis)
            else:
                adjoint = adjoint + curvature(duals[axis], axis)
        updated = (field - step_primal * adjoint + step_primal * target) / (1.0 + step_primal)
        lead = 2.0 * updated - field
        field = updated
    return (field, duals)


def z_tables(length):
    half = length // 2
    position = jnp.arange(length, dtype=jnp.int32)
    column = jnp.arange(length, dtype=jnp.int32)
    is_cosine = column <= half
    frequency = jnp.where(is_cosine, column, column - half)
    phase = position[:, None] * frequency[None, :] % length
    angle = phase.astype(jnp.float32) * (2.0 * math.pi / length)
    forward = jnp.where(is_cosine[None, :], jnp.cos(angle), jnp.sin(angle))
    weight = jnp.where((column == 0) | (column == half), 1.0, 2.0) / length
    backward = forward.T * weight[:, None]
    return (forward, backward)


def x_tables(length):
    half = length // 2
    freqs = jnp.arange(half + 1, dtype=jnp.int32)
    position = jnp.arange(length, dtype=jnp.int32)
    phase = freqs[:, None] * position[None, :] % length
    angle = phase.astype(jnp.float32) * (2.0 * math.pi / length)
    cos_table = jnp.cos(angle)
    sin_table = jnp.sin(angle)
    weight = jnp.where((freqs == 0) | (freqs == half), 1.0, 2.0) / length
    return (cos_table, sin_table, (cos_table * weight[:, None]).T, (sin_table * weight[:, None]).T)


def x_forward(columns, cos_table, sin_table):
    flat = columns.reshape(columns.shape[0], -1)
    shape_out = (cos_table.shape[0],) + columns.shape[1:]
    real_part = jnp.dot(cos_table, flat, precision=highest).reshape(shape_out)
    imag_part = jnp.dot(sin_table, flat, precision=highest).reshape(shape_out)
    return (real_part, imag_part)


def x_inverse(real_part, imag_part, cos_back, sin_back):
    rows = real_part.shape[0]
    flat_real = real_part.reshape(rows, -1)
    flat_imag = imag_part.reshape(rows, -1)
    summed = jnp.dot(cos_back, flat_real, precision=highest) + jnp.dot(
        sin_back, flat_imag, precision=highest
    )
    return summed.reshape((cos_back.shape[0],) + real_part.shape[1:])


def filters(tf_table, tilt_index, wedge, length_z):
    levels = jnp.arange(tf_table.shape[0], dtype=jnp.int32)
    picked = jnp.sum(jnp.where(tilt_index[:, :, None] == levels, tf_table, 0.0), axis=2)
    half_rows = picked * wedge.astype(jnp.float32)
    response = jnp.concatenate([half_rows, half_rows[:, 1 : length_z // 2]], 1)
    denom = response * response + 1.0
    return ((response / denom)[:, None, :], (1.0 / denom)[:, None, :])


def rim_x_primal(field):
    return extended(field, (("gy", 0),), 1)


def rim_x_dual(field):
    return extended(field, (("gy", 0),), 1)


def local(observed, tf_table, tilt_index, wedge):
    length_z = observed.shape[2]
    forward_z, backward_z = z_tables(length_z)
    cos_table, sin_table, cos_back, sin_back = x_tables(NX)
    g_data, g_prior = filters(tf_table, tilt_index, wedge, length_z)
    packed = jnp.dot(observed, forward_z, precision=highest)
    columns = lax.all_to_all(packed, "gy", split_axis=1, concat_axis=0, tiled=True)
    data_real, data_imag = x_forward(columns, cos_table, sin_table)
    prior_real, prior_imag = (data_real, data_imag)
    current = observed
    duals = (jnp.zeros_like(observed), jnp.zeros_like(observed), jnp.zeros_like(observed))
    for outer in range(OUTER):
        if outer > 0:
            again = lax.all_to_all(
                jnp.dot(current, forward_z, precision=highest),
                "gy",
                split_axis=1,
                concat_axis=0,
                tiled=True,
            )
            prior_real, prior_imag = x_forward(again, cos_table, sin_table)
        merged = x_inverse(
            g_data * data_real + g_prior * prior_real,
            g_data * data_imag + g_prior * prior_imag,
            cos_back,
            sin_back,
        )
        slabs = lax.all_to_all(merged, "gy", split_axis=0, concat_axis=1, tiled=True)
        target = jnp.dot(slabs, backward_z, precision=highest)
        current, duals = denoise(target, duals, 0, rim_x_primal, rim_x_dual)
    return current


def solution(mesh):
    in_specs = (P(("groups", "gy"), None, None), P(), P(), P())
    out_specs = P(("groups", "gy"), None, None)
    return jax.shard_map(local, mesh=mesh, in_specs=in_specs, out_specs=out_specs, check_vma=False)
```

profile of v0, /device:TPU:8, one launch (start us, length us, event | category | flops | bytes accessed | tf_op | source)
XLA Modules:
  0.0 304.0 jit_solution(17991332169227890438)
XLA Ops:
  1.2 3.4 %convolution_bitcast_fusion = f32[64,16,256]{2,0,1:T(8,128)} fusion(f32[64,16,256]{2,1,0:T(8,128)S(1)} %copy-done, s32[256]{0:T(256)S(1)} %add_select_fusion.3, pred[256]{0:T(512)(128)(4,1)S(1)} %iota_compare_fusion.3), kind=kOutput, calls=%fused_computation.55 | convolution fusion | flops 806289408 | bytes 2098432 | tf_op jit(solution)/shard_map/dot_general | solution.py:141
  4.7 6.9 %all-to-all-start = ((f32[64,16,256]{2,0,1:T(8,128)}), f32[64,16,256]{2,0,1:T(8,128)S(1)}, u32[]{:S(2)}, u32[]{:S(2)}) async-start(f32[64,16,256]{2,0,1:T(8,128)} %convolution_bitcast_fusion), calls=%async_computation | async-start | bytes 2097152 | tf_op jit(solution)/shard_map/all_to_all | solution.py:142
  11.6 1.8 select_reduce_fusion
  13.5 21.7 %all-to-all-done = f32[64,16,256]{2,0,1:T(8,128)S(1)} async-done(((f32[64,16,256]{2,0,1:T(8,128)}), f32[64,16,256]{2,0,1:T(8,128)S(1)}, u32[]{:S(2)}, u32[]{:S(2)}) %all-to-all-start) | async-done | bytes 1048608 | tf_op jit(solution)/shard_map/all_to_all | solution.py:142
  35.2 10.8 %fusion.41 = f32[513,256]{0,1:T(8,128)S(1)} fusion(f32[1024,256]{1,0:T(8,128)S(1)} %bitcast.46), kind=kOutput, calls=%fused_computation.67 | convolution fusion | flops 1621112832 | bytes 1573888 | tf_op jit(solution)/shard_map/dot_general | solution.py:105
  46.0 10.5 %fusion.36 = f32[513,256]{0,1:T(8,128)S(1)} fusion(f32[1024,256]{1,0:T(8,128)S(1)} %bitcast.47), kind=kOutput, calls=%fused_computation.66 | convolution fusion | flops 1621112832 | bytes 1573888 | tf_op jit(solution)/shard_map/dot_general | solution.py:104
  56.5 12.6 %fusion.8 = f32[1024,256]{1,0:T(8,128)S(1)} fusion(f32[513]{0:T(1024)S(1)} %select_multiply_fusion.3, f32[513,256]{0,1:T(8,128)S(1)} %fusion.41, f32[513,127]{0,1:T(8,128)S(1)} %slice.276, f32[513,129]{0,1:T(8,128)S(1)} %convert_multiply_fusion), kind=kOutput, calls=%fused_computation.13 | convolution fusion | flops 1622688768 | bytes 2101252 | tf_op jit(solution)/shard_map/dot_general | solution.py:113
  69.1 12.1 %fusion.17 = f32[1024,1,256]{2,0,1:T(8,128)S(1)} fusion(f32[1024,256]{1,0:T(8,128)S(1)} %fusion.8, f32[513]{0:T(1024)S(1)} %select_multiply_fusion.3, f32[513,256]{0,1:T(8,128)S(1)} %fusion.36, f32[513,127]{0,1:T(8,128)S(1)} %slice.276, f32[513,129]{0,1:T(8,128)S(1)} %convert_multiply_fusion), kind=kOutput, calls=%fused_computation.52 | convolution fusion | flops 1622950912 | bytes 3149828 | tf_op jit(solution)/shard_map/dot_general | solution.py:113
  81.2 2.0 copy.43
  83.3 5.6 %all-to-all-start.1 = ((f32[1024,1,256]{2,1,0:T(1,128)}), f32[1024,1,256]{2,1,0:T(1,128)S(1)}, u32[]{:S(2)}, u32[]{:S(2)}) async-start(f32[1024,1,256]{2,1,0:T(1,128)} %copy.43), calls=%async_computation.1 | async-start | bytes 2097152 | tf_op jit(solution)/shard_map/all_to_all | solution.py:163
  88.9 24.1 %all-to-all-done.1 = f32[1024,1,256]{2,1,0:T(1,128)S(1)} async-done(((f32[1024,1,256]{2,1,0:T(1,128)}), f32[1024,1,256]{2,1,0:T(1,128)S(1)}, u32[]{:S(2)}, u32[]{:S(2)}) %all-to-all-start.1) | async-done | bytes 1048608 | tf_op jit(solution)/shard_map/all_to_all | solution.py:163
  113.0 2.6 fusion.146
  115.7 2.5 collective-permute-start
  118.2 2.3 collective-permute-start.1
  120.5 3.7 %collective-permute-done.1 = f32[1,16,256]{2,1,0:T(8,128)S(1)} collective-permute-done((f32[1,16,256]{2,1,0:T(8,128)S(1)}, f32[1,16,256]{2,1,0:T(8,128)S(1)}, u32[]{:S(2)}, u32[]{:S(2)}) %collective-permute-start.1) | collective-permute-done | bytes 16416 | tf_op jit(solution)/shard_map/ppermute | solution.py:24
  125.5 1.9 collective-permute-start.2
  127.4 2.4 collective-permute-start.3
  130.6 2.7 collective-permute-done.3
  134.3 1.9 collective-permute-start.4
  136.3 2.4 collective-permute-start.5
  138.7 3.5 %collective-permute-done.5 = f32[1,16,256]{2,1,0:T(8,128)S(1)} collective-permute-done((f32[1,16,256]{2,1,0:T(8,128)S(1)}, f32[1,16,256]{2,1,0:T(8,128)S(1)}, u32[]{:S(2)}, u32[]{:S(2)}) %collective-permute-start.5) | collective-permute-done | bytes 16416 | tf_op jit(solution)/shard_map/ppermute | solution.py:24
  142.2 1.6 fusion.238
  143.8 1.9 collective-permute-start.6
  145.7 2.4 collective-permute-start.7
  148.6 3.1 %collective-permute-done.7 = f32[1,16,256]{2,1,0:T(8,128)S(1)} collective-permute-done((f32[1,16,256]{2,1,0:T(8,128)S(1)}, f32[1,16,256]{2,1,0:T(8,128)S(1)}, u32[]{:S(2)}, u32[]{:S(2)}) %collective-permute-start.7) | collective-permute-done | bytes 16416 | tf_op jit(solution)/shard_map/ppermute | solution.py:24
  152.7 2.5 fusion.148
  155.3 30.2 %all_to_all.66 = f32[64,16,256]{2,0,1:T(8,128)S(1)} all-to-all(f32[64,16,256]{2,0,1:T(8,128)S(1)} %fusion.148), channel_id=1, replica_groups=mesh['groups'=2,'gy'=16] {'gy'}, dimensions={1} | all-to-all | bytes 2097152 | tf_op jit(solution)/shard_map/all_to_all | solution.py:149
  185.5 10.6 %fusion.26 = f32[513,256]{0,1:T(8,128)S(1)} fusion(f32[1024,256]{1,0:T(8,128)S(1)} %bitcast.48, f32[513,256]{0,1:T(8,128)S(1)} %copy-done.5, f32[513,127]{0,1:T(8,128)S(1)} %slice.276, f32[513,129]{0,1:T(8,128)S(1)} %convert_multiply_fusion), kind=kOutput, calls=%fused_computation.57 | convolution fusion | flops 1622163456 | bytes 2624512 | tf_op jit(solution)/shard_map/dot_general | solution.py:105
  196.1 10.8 %fusion.27 = f32[513,256]{0,1:T(8,128)S(1)} fusion(f32[1024,256]{1,0:T(8,128)S(1)} %bitcast.49, f32[513,256]{0,1:T(8,128)S(1)} %fusion.36, f32[513,127]{0,1:T(8,128)S(1)} %slice.276, f32[513,129]{0,1:T(8,128)S(1)} %convert_multiply_fusion), kind=kOutput, calls=%fused_computation.59 | convolution fusion | flops 1622163456 | bytes 2624512 | tf_op jit(solution)/shard_map/dot_general | solution.py:104
  206.9 12.1 %fusion.6 = f32[1024,256]{1,0:T(8,128)S(1)} fusion(f32[513,256]{0,1:T(8,128)S(1)} %fusion.26, f32[513]{0:T(1024)S(1)} %select_multiply_fusion.3), kind=kOutput, calls=%fused_computation.11 | convolution fusion | flops 1621638144 | bytes 1575940 | tf_op jit(solution)/shard_map/dot_general | solution.py:113
  219.1 12.3 %fusion.23 = f32[1024,1,256]{2,0,1:T(8,128)S(1)} fusion(f32[1024,256]{1,0:T(8,128)S(1)} %fusion.6, f32[513,256]{0,1:T(8,128)S(1)} %fusion.27, f32[513]{0:T(1024)S(1)} %select_multiply_fusion.3), kind=kOutput, calls=%fused_computation.54 | convolution fusion | flops 1621900288 | bytes 2624516 | tf_op jit(solution)/shard_map/dot_general | solution.py:113
  232.6 29.5 %all_to_all.67 = f32[1024,1,256]{2,1,0:T(1,128)S(1)} all-to-all(f32[1024,1,256]{2,1,0:T(1,128)S(1)} %copy.48), channel_id=1, replica_groups=mesh['groups'=2,'gy'=16] {'gy'}, dimensions={0} | all-to-all | bytes 2097152 | tf_op jit(solution)/shard_map/all_to_all | solution.py:163
  262.2 2.6 fusion.144
  264.8 3.2 %collective-permute-start.8 = (f32[1,16,256]{2,1,0:T(8,128)S(1)}, f32[1,16,256]{2,1,0:T(8,128)S(1)}, u32[]{:S(2)}, u32[]{:S(2)}) collective-permute-start(f32[1,16,256]{2,1,0:T(8,128)S(1)} %get-tuple-element.35), channel_id=1, source_target_pairs={{1,0},{2,1},{3,2},{4,3},{5,4},{6,5},{7,6},{8,7},{9,8},{10,9},{11,1... | collective-permute-start | bytes 49160 | tf_op jit(solution)/shard_map/ppermute | solution.py:25
  268.1 1.9 collective-permute-start.9
  270.0 4.0 %collective-permute-done.9 = f32[1,16,256]{2,1,0:T(8,128)S(1)} collective-permute-done((f32[1,16,256]{2,1,0:T(8,128)S(1)}, f32[1,16,256]{2,1,0:T(8,128)S(1)}, u32[]{:S(2)}, u32[]{:S(2)}) %collective-permute-start.9) | collective-permute-done | bytes 16416 | tf_op jit(solution)/shard_map/ppermute | solution.py:24
  274.1 1.6 fusion.239
  275.6 1.9 collective-permute-start.10
  277.6 2.4 collective-permute-start.11
  280.4 3.1 %collective-permute-done.11 = f32[1,16,256]{2,1,0:T(8,128)S(1)} collective-permute-done((f32[1,16,256]{2,1,0:T(8,128)S(1)}, f32[1,16,256]{2,1,0:T(8,128)S(1)}, u32[]{:S(2)}, u32[]{:S(2)}) %collective-permute-start.11) | collective-permute-done | bytes 16416 | tf_op jit(solution)/shard_map/ppermute | solution.py:24
  284.5 1.9 collective-permute-start.12
  286.4 2.4 collective-permute-start.13
  288.8 3.5 %collective-permute-done.13 = f32[1,16,256]{2,1,0:T(8,128)S(1)} collective-permute-done((f32[1,16,256]{2,1,0:T(8,128)S(1)}, f32[1,16,256]{2,1,0:T(8,128)S(1)}, u32[]{:S(2)}, u32[]{:S(2)}) %collective-permute-start.13) | collective-permute-done | bytes 16416 | tf_op jit(solution)/shard_map/ppermute | solution.py:24
  292.4 1.6 fusion.240
  293.9 1.9 collective-permute-start.14
  295.9 2.4 collective-permute-start.15
  298.7 3.1 %collective-permute-done.15 = f32[1,16,256]{2,1,0:T(8,128)S(1)} collective-permute-done((f32[1,16,256]{2,1,0:T(8,128)S(1)}, f32[1,16,256]{2,1,0:T(8,128)S(1)}, u32[]{:S(2)}, u32[]{:S(2)}) %collective-permute-start.15) | collective-permute-done | bytes 16416 | tf_op jit(solution)/shard_map/ppermute | solution.py:24
  301.8 2.0 fusion.115
  (45 shorter events, 9.1 us)
Async XLA Ops:
  0.0 1.2 copy-start
  4.7 6.9 %copy-start.1 = (s32[513,129]{0,1:T(8,128)S(1)}, s32[513,129]{0,1:T(8,128)}, u32[]{:S(2)}) copy-start(s32[513,129]{0,1:T(8,128)} %param.6) | copy-start | bytes 794128
  4.7 6.9 %copy-start.3 = (f32[16]{0:T(128)S(1)}, f32[16]{0:T(128)}, u32[]{:S(2)}) copy-start(f32[16]{0:T(128)} %param.5) | copy-start | bytes 196
  4.7 8.7 %copy-start.2 = (s32[513,129]{0,1:T(8,128)S(1)}, s32[513,129]{0,1:T(8,128)}, u32[]{:S(2)}) copy-start(s32[513,129]{0,1:T(8,128)} %param.7) | copy-start | bytes 794128
  4.7 30.5 %all-to-all-start = ((f32[64,16,256]{2,0,1:T(8,128)}), f32[64,16,256]{2,0,1:T(8,128)S(1)}, u32[]{:S(2)}, u32[]{:S(2)}) async-start(f32[64,16,256]{2,0,1:T(8,128)} %convolution_bitcast_fusion), calls=%async_computation | async-start | bytes 2097152 | tf_op jit(solution)/shard_map/all_to_all | solution.py:142
  46.0 10.5 %copy-start.4 = (f32[513,256]{0,1:T(8,128)}, f32[513,256]{0,1:T(8,128)S(1)}, u32[]{:S(2)}) copy-start(f32[513,256]{0,1:T(8,128)S(1)} %fusion.41) | copy-start | bytes 1575940
  83.3 29.7 %all-to-all-start.1 = ((f32[1024,1,256]{2,1,0:T(1,128)}), f32[1024,1,256]{2,1,0:T(1,128)S(1)}, u32[]{:S(2)}, u32[]{:S(2)}) async-start(f32[1024,1,256]{2,1,0:T(1,128)} %copy.43), calls=%async_computation.1 | async-start | bytes 2097152 | tf_op jit(solution)/shard_map/all_to_all | solution.py:163
  115.7 4.8 %collective-permute-start = (f32[1,16,256]{2,1,0:T(8,128)S(1)}, f32[1,16,256]{2,1,0:T(8,128)S(1)}, u32[]{:S(2)}, u32[]{:S(2)}) collective-permute-start(f32[1,16,256]{2,1,0:T(8,128)S(1)} %get-tuple-element.45), channel_id=1, source_target_pairs={{1,0},{2,1},{3,2},{4,3},{5,4},{6,5},{7,6},{8,7},{9,8},{10,9},{11,1... | collective-permute-start | bytes 49160 | tf_op jit(solution)/shard_map/ppermute | solution.py:25
  118.2 6.0 %collective-permute-start.1 = (f32[1,16,256]{2,1,0:T(8,128)S(1)}, f32[1,16,256]{2,1,0:T(8,128)S(1)}, u32[]{:S(2)}, u32[]{:S(2)}) collective-permute-start(f32[1,16,256]{2,1,0:T(8,128)S(1)} %get-tuple-element.46), channel_id=1, source_target_pairs={{0,1},{1,2},{2,3},{3,4},{4,5},{5,6},{6,7},{7,8},{8,9},{9,10},{10,1... | collective-permute-start | bytes 49160 | tf_op jit(solution)/shard_map/ppermute | solution.py:24
  125.5 5.1 %collective-permute-start.2 = (f32[1,16,256]{2,1,0:T(8,128)S(1)}, f32[1,16,256]{2,1,0:T(8,128)S(1)}, u32[]{:S(2)}, u32[]{:S(2)}) collective-permute-start(f32[1,16,256]{2,1,0:T(8,128)S(1)} %get-tuple-element.43), channel_id=1, source_target_pairs={{1,0},{2,1},{3,2},{4,3},{5,4},{6,5},{7,6},{8,7},{9,8},{10,9},{11,1... | collective-permute-start | bytes 49160 | tf_op jit(solution)/shard_map/ppermute | solution.py:25
  127.4 6.0 %collective-permute-start.3 = (f32[1,16,256]{2,1,0:T(8,128)S(1)}, f32[1,16,256]{2,1,0:T(8,128)S(1)}, u32[]{:S(2)}, u32[]{:S(2)}) collective-permute-start(f32[1,16,256]{2,1,0:T(8,128)S(1)} %get-tuple-element.44), channel_id=1, source_target_pairs={{0,1},{1,2},{2,3},{3,4},{4,5},{5,6},{6,7},{7,8},{8,9},{9,10},{10,1... | collective-permute-start | bytes 49160 | tf_op jit(solution)/shard_map/ppermute | solution.py:24
  134.3 4.3 %collective-permute-start.4 = (f32[1,16,256]{2,1,0:T(8,128)S(1)}, f32[1,16,256]{2,1,0:T(8,128)S(1)}, u32[]{:S(2)}, u32[]{:S(2)}) collective-permute-start(f32[1,16,256]{2,1,0:T(8,128)S(1)} %get-tuple-element.41), channel_id=1, source_target_pairs={{1,0},{2,1},{3,2},{4,3},{5,4},{6,5},{7,6},{8,7},{9,8},{10,9},{11,1... | collective-permute-start | bytes 49160 | tf_op jit(solution)/shard_map/ppermute | solution.py:25
  136.3 6.0 %collective-permute-start.5 = (f32[1,16,256]{2,1,0:T(8,128)S(1)}, f32[1,16,256]{2,1,0:T(8,128)S(1)}, u32[]{:S(2)}, u32[]{:S(2)}) collective-permute-start(f32[1,16,256]{2,1,0:T(8,128)S(1)} %get-tuple-element.42), channel_id=1, source_target_pairs={{0,1},{1,2},{2,3},{3,4},{4,5},{5,6},{6,7},{7,8},{8,9},{9,10},{10,1... | collective-permute-start | bytes 49160 | tf_op jit(solution)/shard_map/ppermute | solution.py:24
  143.8 4.8 %collective-permute-start.6 = (f32[1,16,256]{2,1,0:T(8,128)S(1)}, f32[1,16,256]{2,1,0:T(8,128)S(1)}, u32[]{:S(2)}, u32[]{:S(2)}) collective-permute-start(f32[1,16,256]{2,1,0:T(8,128)S(1)} %get-tuple-element.37), channel_id=1, source_target_pairs={{1,0},{2,1},{3,2},{4,3},{5,4},{6,5},{7,6},{8,7},{9,8},{10,9},{11,1... | collective-permute-start | bytes 49160 | tf_op jit(solution)/shard_map/ppermute | solution.py:25
  145.7 6.0 %collective-permute-start.7 = (f32[1,16,256]{2,1,0:T(8,128)S(1)}, f32[1,16,256]{2,1,0:T(8,128)S(1)}, u32[]{:S(2)}, u32[]{:S(2)}) collective-permute-start(f32[1,16,256]{2,1,0:T(8,128)S(1)} %get-tuple-element.38), channel_id=1, source_target_pairs={{0,1},{1,2},{2,3},{3,4},{4,5},{5,6},{6,7},{7,8},{8,9},{9,10},{10,1... | collective-permute-start | bytes 49160 | tf_op jit(solution)/shard_map/ppermute | solution.py:24
  155.3 30.2 %copy-start.5 = (f32[513,256]{0,1:T(8,128)S(1)}, f32[513,256]{0,1:T(8,128)}, u32[]{:S(2)}) copy-start(f32[513,256]{0,1:T(8,128)} %copy-done.4) | copy-start | bytes 1575940
  264.8 5.2 %collective-permute-start.8 = (f32[1,16,256]{2,1,0:T(8,128)S(1)}, f32[1,16,256]{2,1,0:T(8,128)S(1)}, u32[]{:S(2)}, u32[]{:S(2)}) collective-permute-start(f32[1,16,256]{2,1,0:T(8,128)S(1)} %get-tuple-element.35), channel_id=1, source_target_pairs={{1,0},{2,1},{3,2},{4,3},{5,4},{6,5},{7,6},{8,7},{9,8},{10,9},{11,1... | collective-permute-start | bytes 49160 | tf_op jit(solution)/shard_map/ppermute | solution.py:25
  268.1 6.0 %collective-permute-start.9 = (f32[1,16,256]{2,1,0:T(8,128)S(1)}, f32[1,16,256]{2,1,0:T(8,128)S(1)}, u32[]{:S(2)}, u32[]{:S(2)}) collective-permute-start(f32[1,16,256]{2,1,0:T(8,128)S(1)} %get-tuple-element.36), channel_id=1, source_target_pairs={{0,1},{1,2},{2,3},{3,4},{4,5},{5,6},{6,7},{7,8},{8,9},{9,10},{10,1... | collective-permute-start | bytes 49160 | tf_op jit(solution)/shard_map/ppermute | solution.py:24
  275.6 4.8 %collective-permute-start.10 = (f32[1,16,256]{2,1,0:T(8,128)S(1)}, f32[1,16,256]{2,1,0:T(8,128)S(1)}, u32[]{:S(2)}, u32[]{:S(2)}) collective-permute-start(f32[1,16,256]{2,1,0:T(8,128)S(1)} %get-tuple-element.31), channel_id=1, source_target_pairs={{1,0},{2,1},{3,2},{4,3},{5,4},{6,5},{7,6},{8,7},{9,8},{10,9},{11,1... | collective-permute-start | bytes 49160 | tf_op jit(solution)/shard_map/ppermute | solution.py:25
  277.6 6.0 %collective-permute-start.11 = (f32[1,16,256]{2,1,0:T(8,128)S(1)}, f32[1,16,256]{2,1,0:T(8,128)S(1)}, u32[]{:S(2)}, u32[]{:S(2)}) collective-permute-start(f32[1,16,256]{2,1,0:T(8,128)S(1)} %get-tuple-element.32), channel_id=1, source_target_pairs={{0,1},{1,2},{2,3},{3,4},{4,5},{5,6},{6,7},{7,8},{8,9},{9,10},{10,1... | collective-permute-start | bytes 49160 | tf_op jit(solution)/shard_map/ppermute | solution.py:24
  284.5 4.3 %collective-permute-start.12 = (f32[1,16,256]{2,1,0:T(8,128)S(1)}, f32[1,16,256]{2,1,0:T(8,128)S(1)}, u32[]{:S(2)}, u32[]{:S(2)}) collective-permute-start(f32[1,16,256]{2,1,0:T(8,128)S(1)} %get-tuple-element.29), channel_id=1, source_target_pairs={{1,0},{2,1},{3,2},{4,3},{5,4},{6,5},{7,6},{8,7},{9,8},{10,9},{11,1... | collective-permute-start | bytes 49160 | tf_op jit(solution)/shard_map/ppermute | solution.py:25
  286.4 6.0 %collective-permute-start.13 = (f32[1,16,256]{2,1,0:T(8,128)S(1)}, f32[1,16,256]{2,1,0:T(8,128)S(1)}, u32[]{:S(2)}, u32[]{:S(2)}) collective-permute-start(f32[1,16,256]{2,1,0:T(8,128)S(1)} %get-tuple-element.30), channel_id=1, source_target_pairs={{0,1},{1,2},{2,3},{3,4},{4,5},{5,6},{6,7},{7,8},{8,9},{9,10},{10,1... | collective-permute-start | bytes 49160 | tf_op jit(solution)/shard_map/ppermute | solution.py:24
  293.9 4.8 %collective-permute-start.14 = (f32[1,16,256]{2,1,0:T(8,128)S(1)}, f32[1,16,256]{2,1,0:T(8,128)S(1)}, u32[]{:S(2)}, u32[]{:S(2)}) collective-permute-start(f32[1,16,256]{2,1,0:T(8,128)S(1)} %get-tuple-element.25), channel_id=1, source_target_pairs={{1,0},{2,1},{3,2},{4,3},{5,4},{6,5},{7,6},{8,7},{9,8},{10,9},{11,1... | collective-permute-start | bytes 49160 | tf_op jit(solution)/shard_map/ppermute | solution.py:25
  295.9 6.0 %collective-permute-start.15 = (f32[1,16,256]{2,1,0:T(8,128)S(1)}, f32[1,16,256]{2,1,0:T(8,128)S(1)}, u32[]{:S(2)}, u32[]{:S(2)}) collective-permute-start(f32[1,16,256]{2,1,0:T(8,128)S(1)} %get-tuple-element.26), channel_id=1, source_target_pairs={{0,1},{1,2},{2,3},{3,4},{4,5},{5,6},{6,7},{7,8},{8,9},{9,10},{10,1... | collective-permute-start | bytes 49160 | tf_op jit(solution)/shard_map/ppermute | solution.py:24
where the time goes:
time: 307 us; the launch traced here: 304 us
  matrix products  103 us (34%)
  waiting for transfers between devices  72.6 us (24%)
  blocking collectives  59.7 us (19%)
  starting transfers between devices  48.4 us (16%)
  other arithmetic  14.8 us (5%)
  local copies, waits for them, and re-layouts  4.73 us (2%)
    all_to_all x1, blocking collectives, local(): lax.all_to_all(jnp.dot(current, forward_z, precision=highest), 'gy', spli...  30.2 us
    all_to_all x1, blocking collectives, local(): lax.all_to_all(merged, 'gy', split_axis=0, concat_axis=1, tiled=True)  29.5 us
    ppermute x8, waiting for transfers between devices, extended(): before = lax.ppermute(last, axis, up)  26.8 us
    dot_general x2, matrix products, x_inverse(): jnp.dot(sin_back, flat_imag, precision=highest)  24.8 us
    dot_general x2, matrix products, x_inverse(): jnp.dot(cos_back, flat_real, precision=highest)  24.4 us
    all_to_all x1, waiting for transfers between devices, local(): lax.all_to_all(merged, 'gy', split_axis=0, concat_axis=1, tiled=True)  24.1 us
    all_to_all x1, waiting for transfers between devices, local(): lax.all_to_all(packed, 'gy', split_axis=1, concat_axis=0, tiled=True)  21.7 us
    dot_general x2, matrix products, x_forward(): imag_part = jnp.dot(sin_table, flat, precision=highest).reshape(shape_out)  21.4 us
  transfers between devices with their start and end apart: 18, of which 10 were waited for; matrix products, arithmetic and copies ran while one was open for 1% of the time, Pallas kernels for 0%

commit v1 on v0

--- a/solution.py
+++ b/solution.py
@@ -12,6 +12,18 @@
 huber_eps = 0.05
 bound_dual = 0.5
 highest = lax.Precision.HIGHEST
+
+
+def in_blocks(value, dim, size):
+    shape = value.shape
+    parts = value.reshape(*shape[:dim], size, shape[dim] // size, *shape[dim + 1 :])
+    return jnp.moveaxis(parts, dim, 0)
+
+
+def laid_out(blocks, dim):
+    blocks = jnp.moveaxis(blocks, 0, dim)
+    lengths = blocks.shape
+    return blocks.reshape(*lengths[:dim], lengths[dim] * lengths[dim + 1], *lengths[dim + 2 :])
 
 
 def extended(value, sides, width):
@@ -146,13 +158,15 @@
     duals = (jnp.zeros_like(observed), jnp.zeros_like(observed), jnp.zeros_like(observed))
     for outer in range(OUTER):
         if outer > 0:
-            again = lax.all_to_all(
-                jnp.dot(current, forward_z, precision=highest),
-                "gy",
-                split_axis=1,
-                concat_axis=0,
-                tiled=True,
-            )
+            x = jnp.dot(current, forward_z, precision=highest)
+            size, position_2 = (lax.axis_size("gy"), lax.axis_index("gy"))
+            tiles = in_blocks(x, 1, size)
+            outs = [tiles[position_2]]
+            for hop in range(1, size):
+                sent = tiles[position_2 ^ hop]
+                outs.append(lax.ppermute(sent, "gy", [(i_2, i_2 ^ hop) for i_2 in range(size)]))
+            tiles = jnp.stack(outs)[position_2 ^ jnp.arange(size)]
+            again = laid_out(tiles, 0)
             prior_real, prior_imag = x_forward(again, cos_table, sin_table)
         merged = x_inverse(
             g_data * data_real + g_prior * prior_real,

time: 307 us -> 322 us (1.049)
  blocking collectives: 59.7 us -> 28.7 us
  starting transfers between devices: 48.4 us -> 65.9 us
  waiting for transfers between devices: 72.6 us -> 88.5 us
  local copies, waits for them, and re-layouts: 4.73 us -> 9.8 us
  other arithmetic: 14.8 us -> 19.1 us
    all_to_all x1 -> x0, blocking collectives: 30.2 us -> none  [local(): lax.all_to_all(jnp.dot(current, forward_z, precision=highest), 'gy', spli...]
    ppermute x0 -> x15, starting transfers between devices: none -> 17.2 us  [local(): lax.ppermute(sent, 'gy', [(i_2, i_2 ^ hop) for i_2 in range(size)])]
    ppermute x0 -> x15, waiting for transfers between devices: none -> 16.3 us  [local(): lax.ppermute(sent, 'gy', [(i_2, i_2 ^ hop) for i_2 in range(size)])]
    div x8, other arithmetic: 8.02 us -> 12.5 us  [denoise(): duals = (raised[0] / shrink, raised[1] / shrink, raised[2] / shrink)]
  transfers between devices with their start and end apart: 18 -> 33, of which waited for: 10 -> 18; matrix products, arithmetic and copies ran while one was open for 1% -> 1% of each run, Pallas kernels for 0% -> 0%
where the time goes in v1:
time: 322 us; the launch traced here: 318 us
  matrix products  105 us (33%)
  waiting for transfers between devices  88.5 us (27%)
  starting transfers between devices  65.9 us (20%)
  blocking collectives  28.7 us (9%)
  other arithmetic  19.1 us (6%)
  local copies, waits for them, and re-layouts  9.8 us (3%)
    all_to_all x1, blocking collectives, local(): lax.all_to_all(merged, 'gy', split_axis=0, concat_axis=1, tiled=True)  28.7 us
    ppermute x8, waiting for transfers between devices, extended(): before = lax.ppermute(last, axis, up)  26.1 us
    dot_general x2, matrix products, x_inverse(): jnp.dot(sin_back, flat_imag, precision=highest)  24.8 us
    dot_general x2, matrix products, x_inverse(): jnp.dot(cos_back, flat_real, precision=highest)  24.2 us
    all_to_all x1, waiting for transfers between devices, local(): lax.all_to_all(merged, 'gy', split_axis=0, concat_axis=1, tiled=True)  24.1 us
    dot_general x2, matrix products, x_forward(): real_part = jnp.dot(cos_table, flat, precision=highest).reshape(shape_out)  23 us
    all_to_all x1, waiting for transfers between devices, local(): lax.all_to_all(packed, 'gy', split_axis=1, concat_axis=0, tiled=True)  22 us
    dot_general x2, matrix products, x_forward(): imag_part = jnp.dot(sin_table, flat, precision=highest).reshape(shape_out)  21.8 us
  transfers between devices with their start and end apart: 33, of which 18 were waited for; matrix products, arithmetic and copies ran while one was open for 1% of the time, Pallas kernels for 0%

profile of v1, /device:TPU:8, one launch (start us, length us, event | category | flops | bytes accessed | tf_op | source)
XLA Modules:
  0.0 318.1 jit_solution(4752081651464430529)
XLA Ops:
  1.2 3.4 %convolution_bitcast_fusion = f32[64,16,256]{2,0,1:T(8,128)} fusion(f32[64,16,256]{2,1,0:T(8,128)S(1)} %copy-done, s32[256]{0:T(256)S(1)} %add_select_fusion.3, pred[256]{0:T(512)(128)(4,1)S(1)} %iota_compare_fusion.3), kind=kOutput, calls=%fused_computation.56 | convolution fusion | flops 806289408 | bytes 2098432 | tf_op jit(solution)/shard_map/dot_general | solution.py:153
  4.7 6.6 %all-to-all-start = ((f32[64,16,256]{2,0,1:T(8,128)}), f32[64,16,256]{2,0,1:T(8,128)S(1)}, u32[]{:S(2)}, u32[]{:S(2)}) async-start(f32[64,16,256]{2,0,1:T(8,128)} %convolution_bitcast_fusion), calls=%async_computation | async-start | bytes 2097152 | tf_op jit(solution)/shard_map/all_to_all | solution.py:154
  13.2 22.0 %all-to-all-done = f32[64,16,256]{2,0,1:T(8,128)S(1)} async-done(((f32[64,16,256]{2,0,1:T(8,128)}), f32[64,16,256]{2,0,1:T(8,128)S(1)}, u32[]{:S(2)}, u32[]{:S(2)}) %all-to-all-start) | async-done | bytes 1048608 | tf_op jit(solution)/shard_map/all_to_all | solution.py:154
  35.2 10.9 %fusion.41 = f32[513,256]{0,1:T(8,128)S(1)} fusion(f32[1024,256]{1,0:T(8,128)S(1)} %bitcast.82), kind=kOutput, calls=%fused_computation.68 | convolution fusion | flops 1621112832 | bytes 1573888 | tf_op jit(solution)/shard_map/dot_general | solution.py:117
  46.1 10.7 %fusion.36 = f32[513,256]{0,1:T(8,128)S(1)} fusion(f32[1024,256]{1,0:T(8,128)S(1)} %bitcast.83), kind=kOutput, calls=%fused_computation.67 | convolution fusion | flops 1621112832 | bytes 1573888 | tf_op jit(solution)/shard_map/dot_general | solution.py:116
  56.8 12.5 %fusion.8 = f32[1024,256]{1,0:T(8,128)S(1)} fusion(f32[513]{0:T(1024)S(1)} %select_multiply_fusion.3, f32[513,256]{0,1:T(8,128)S(1)} %fusion.41, f32[513,127]{0,1:T(8,128)S(1)} %slice.278, f32[513,129]{0,1:T(8,128)S(1)} %convert_multiply_fusion), kind=kOutput, calls=%fused_computation.14 | convolution fusion | flops 1622688768 | bytes 2101252 | tf_op jit(solution)/shard_map/dot_general | solution.py:125
  69.4 12.1 %fusion.17 = f32[1024,1,256]{2,0,1:T(8,128)S(1)} fusion(f32[1024,256]{1,0:T(8,128)S(1)} %fusion.8, f32[513]{0:T(1024)S(1)} %select_multiply_fusion.3, f32[513,256]{0,1:T(8,128)S(1)} %fusion.36, f32[513,127]{0,1:T(8,128)S(1)} %slice.278, f32[513,129]{0,1:T(8,128)S(1)} %convert_multiply_fusion), kind=kOutput, calls=%fused_computation.53 | convolution fusion | flops 1622950912 | bytes 3149828 | tf_op jit(solution)/shard_map/dot_general | solution.py:125
  81.5 2.0 copy.34
  83.5 5.6 %all-to-all-start.1 = ((f32[1024,1,256]{2,1,0:T(1,128)}), f32[1024,1,256]{2,1,0:T(1,128)S(1)}, u32[]{:S(2)}, u32[]{:S(2)}) async-start(f32[1024,1,256]{2,1,0:T(1,128)} %copy.34), calls=%async_computation.1 | async-start | bytes 2097152 | tf_op jit(solution)/shard_map/all_to_all | solution.py:177
  89.2 24.1 %all-to-all-done.1 = f32[1024,1,256]{2,1,0:T(1,128)S(1)} async-done(((f32[1024,1,256]{2,1,0:T(1,128)}), f32[1024,1,256]{2,1,0:T(1,128)S(1)}, u32[]{:S(2)}, u32[]{:S(2)}) %all-to-all-start.1) | async-done | bytes 1048608 | tf_op jit(solution)/shard_map/all_to_all | solution.py:177
  113.3 2.6 fusion.152
  115.9 2.5 collective-permute-start
  118.5 2.3 collective-permute-start.1
  120.8 3.7 %collective-permute-done.1 = f32[1,16,256]{2,1,0:T(8,128)S(1)} collective-permute-done((f32[1,16,256]{2,1,0:T(8,128)S(1)}, f32[1,16,256]{2,1,0:T(8,128)S(1)}, u32[]{:S(2)}, u32[]{:S(2)}) %collective-permute-start.1) | collective-permute-done | bytes 16416 | tf_op jit(solution)/shard_map/ppermute | solution.py:36
  125.7 1.9 collective-permute-start.2
  127.7 2.4 collective-permute-start.3
  130.9 2.7 collective-permute-done.3
  139.0 2.4 collective-permute-start.5
  141.6 3.4 %collective-permute-done.5 = f32[1,16,256]{2,1,0:T(8,128)S(1)} collective-permute-done((f32[1,16,256]{2,1,0:T(8,128)S(1)}, f32[1,16,256]{2,1,0:T(8,128)S(1)}, u32[]{:S(2)}, u32[]{:S(2)}) %collective-permute-start.5) | collective-permute-done | bytes 16416 | tf_op jit(solution)/shard_map/ppermute | solution.py:36
  145.0 6.1 %fusion.256 = (f32[64,16,256]{2,1,0:T(8,128)S(1)}, f32[64,16,256]{2,1,0:T(8,128)S(1)}, f32[64,16,256]{2,1,0:T(8,128)S(1)}, f32[64,16,256]{2,1,0:T(8,128)S(1)}) fusion(f32[64,16,256]{2,1,0:T(8,128)S(1)} %get-tuple-element.21, f32[64,16,256]{2,1,0:T(8,128)} %copy-done.3, f32[1,16,256]{2,1,0:T(8,128)S(1)} %collective-permute-done.5, ...), kind=kLoop, calls=%fused_computation.347 | loop fusion | flops 6815744 | bytes 8421376 | tf_op jit(solution)/shard_map/div | solution.py:73
  151.1 1.9 collective-permute-start.6
  153.0 2.8 collective-permute-start.7
  156.2 2.7 collective-permute-done.7
  159.0 2.7 fusion.77
  162.9 2.1 collective-permute-start.9
  169.7 2.1 collective-permute-start.15
  172.2 3.5 %collective-permute-start.17 = (f32[64,1,256]{2,1,0:T(1,128)S(1)}, f32[64,1,256]{2,1,0:T(1,128)S(1)}, u32[]{:S(2)}, u32[]{:S(2)}) collective-permute-start(f32[64,1,256]{2,1,0:T(1,128)S(1)} %get-tuple-element.42), channel_id=1, source_target_pairs={{0,10},{1,11},{2,8},{3,9},{4,14},{5,15},{6,12},{7,13},{8,2},{9,3},... | collective-permute-start | bytes 196616 | tf_op jit(solution)/shard_map/ppermute | solution.py:167
  176.2 2.6 collective-permute-start.19
  179.8 3.6 %collective-permute-done.16 = f32[64,1,256]{2,1,0:T(1,128)S(1)} collective-permute-done((f32[64,1,256]{2,1,0:T(1,128)S(1)}, f32[64,1,256]{2,1,0:T(1,128)S(1)}, u32[]{:S(2)}, u32[]{:S(2)}) %collective-permute-start.16) | collective-permute-done | bytes 65568 | tf_op jit(solution)/shard_map/ppermute | solution.py:167
  186.9 4.1 %collective-permute-done.19 = f32[64,1,256]{2,1,0:T(1,128)S(1)} collective-permute-done((f32[64,1,256]{2,1,0:T(1,128)S(1)}, f32[64,1,256]{2,1,0:T(1,128)S(1)}, u32[]{:S(2)}, u32[]{:S(2)}) %collective-permute-start.19) | collective-permute-done | bytes 65568 | tf_op jit(solution)/shard_map/ppermute | solution.py:167
  192.4 2.8 collective-permute-done.21
  198.4 12.3 %fusion.27 = f32[513,256]{0,1:T(8,128)S(1)} fusion(f32[1024,256]{1,0:T(8,128)} %bitcast.80, f32[513,256]{0,1:T(8,128)} %copy-done.21, f32[513,127]{0,1:T(8,128)} %copy-done.12, f32[513,129]{0,1:T(8,128)S(1)} %convert_multiply_fusion), kind=kOutput, calls=%fused_computation.60 | convolution fusion | flops 1622163456 | bytes 2624512 | tf_op jit(solution)/shard_map/dot_general | solution.py:116
  210.7 10.8 %fusion.26 = f32[513,256]{0,1:T(8,128)S(1)} fusion(f32[1024,256]{1,0:T(8,128)S(1)} %bitcast.81, f32[513,256]{0,1:T(8,128)S(1)} %copy-done.20, f32[513,127]{0,1:T(8,128)S(1)} %copy-done.13, f32[513,129]{0,1:T(8,128)S(1)} %convert_multiply_fusion), kind=kOutput, calls=%fused_computation.58 | convolution fusion | flops 1622163456 | bytes 2624512 | tf_op jit(solution)/shard_map/dot_general | solution.py:117
  221.6 12.3 %fusion.6 = f32[1024,256]{1,0:T(8,128)S(1)} fusion(f32[513,256]{0,1:T(8,128)S(1)} %fusion.26, f32[513]{0:T(1024)S(1)} %copy-done.17), kind=kOutput, calls=%fused_computation.12 | convolution fusion | flops 1621638144 | bytes 1575940 | tf_op jit(solution)/shard_map/dot_general | solution.py:125
  233.9 12.1 %fusion.23 = f32[1024,1,256]{2,0,1:T(8,128)S(1)} fusion(f32[1024,256]{1,0:T(8,128)S(1)} %fusion.6, f32[513,256]{0,1:T(8,128)S(1)} %fusion.27, f32[513]{0:T(1024)S(1)} %copy-done.17), kind=kOutput, calls=%fused_computation.55 | convolution fusion | flops 1621900288 | bytes 2624516 | tf_op jit(solution)/shard_map/dot_general | solution.py:125
  247.1 28.7 %all_to_all.51 = f32[1024,1,256]{2,1,0:T(1,128)S(1)} all-to-all(f32[1024,1,256]{2,1,0:T(1,128)S(1)} %copy.38), channel_id=1, replica_groups=mesh['groups'=2,'gy'=16] {'gy'}, dimensions={0} | all-to-all | bytes 2097152 | tf_op jit(solution)/shard_map/all_to_all | solution.py:177
  276.4 2.6 fusion.150
  279.0 3.2 %collective-permute-start.23 = (f32[1,16,256]{2,1,0:T(8,128)S(1)}, f32[1,16,256]{2,1,0:T(8,128)S(1)}, u32[]{:S(2)}, u32[]{:S(2)}) collective-permute-start(f32[1,16,256]{2,1,0:T(8,128)S(1)} %get-tuple-element.35), channel_id=1, source_target_pairs={{1,0},{2,1},{3,2},{4,3},{5,4},{6,5},{7,6},{8,7},{9,8},{10,9},{11,1... | collective-permute-start | bytes 49160 | tf_op jit(solution)/shard_map/ppermute | solution.py:37
  282.3 1.9 collective-permute-start.24
  284.2 4.0 %collective-permute-done.24 = f32[1,16,256]{2,1,0:T(8,128)S(1)} collective-permute-done((f32[1,16,256]{2,1,0:T(8,128)S(1)}, f32[1,16,256]{2,1,0:T(8,128)S(1)}, u32[]{:S(2)}, u32[]{:S(2)}) %collective-permute-start.24) | collective-permute-done | bytes 16416 | tf_op jit(solution)/shard_map/ppermute | solution.py:36
  289.8 1.9 collective-permute-start.25
  291.7 2.6 collective-permute-start.26
  294.8 2.9 collective-permute-done.26
  300.6 2.4 collective-permute-start.28
  303.0 3.5 %collective-permute-done.28 = f32[1,16,256]{2,1,0:T(8,128)S(1)} collective-permute-done((f32[1,16,256]{2,1,0:T(8,128)S(1)}, f32[1,16,256]{2,1,0:T(8,128)S(1)}, u32[]{:S(2)}, u32[]{:S(2)}) %collective-permute-start.28) | collective-permute-done | bytes 16416 | tf_op jit(solution)/shard_map/ppermute | solution.py:36
  310.0 2.4 collective-permute-start.30
  312.9 3.1 collective-permute-done.30
  316.0 1.9 fusion.118
  (126 shorter events, 37.2 us)
Async XLA Ops:
  4.7 6.6 %copy-start.10 = (s32[513,129]{0,1:T(8,128)S(1)}, s32[513,129]{0,1:T(8,128)}, u32[]{:S(2)}) copy-start(s32[513,129]{0,1:T(8,128)} %param.6) | copy-start | bytes 794128
  4.7 6.6 %copy-start.18 = (f32[16]{0:T(128)S(1)}, f32[16]{0:T(128)}, u32[]{:S(2)}) copy-start(f32[16]{0:T(128)} %param.5) | copy-start | bytes 196
  4.7 8.4 %copy-start.11 = (s32[513,129]{0,1:T(8,128)S(1)}, s32[513,129]{0,1:T(8,128)}, u32[]{:S(2)}) copy-start(s32[513,129]{0,1:T(8,128)} %param.7) | copy-start | bytes 794128
  4.7 30.5 %all-to-all-start = ((f32[64,16,256]{2,0,1:T(8,128)}), f32[64,16,256]{2,0,1:T(8,128)S(1)}, u32[]{:S(2)}, u32[]{:S(2)}) async-start(f32[64,16,256]{2,0,1:T(8,128)} %convolution_bitcast_fusion), calls=%async_computation | async-start | bytes 2097152 | tf_op jit(solution)/shard_map/all_to_all | solution.py:154
  13.2 56.2 %copy-start.12 = (f32[513,127]{0,1:T(8,128)}, f32[513,127]{0,1:T(8,128)S(1)}, u32[]{:S(2)}) copy-start(f32[513,127]{0,1:T(8,128)S(1)} %slice.278) | copy-start | bytes 781816
  13.2 56.2 %copy-start.16 = (f32[513]{0:T(1024)}, f32[513]{0:T(1024)S(1)}, u32[]{:S(2)}) copy-start(f32[513]{0:T(1024)S(1)} %select_multiply_fusion.3) | copy-start | bytes 6160
  46.1 10.7 %copy-start.19 = (f32[513,256]{0,1:T(8,128)}, f32[513,256]{0,1:T(8,128)S(1)}, u32[]{:S(2)}) copy-start(f32[513,256]{0,1:T(8,128)S(1)} %fusion.41) | copy-start | bytes 1575940
  56.8 12.6 %copy-start.21 = (f32[513,256]{0,1:T(8,128)}, f32[513,256]{0,1:T(8,128)S(1)}, u32[]{:S(2)}) copy-start(f32[513,256]{0,1:T(8,128)S(1)} %fusion.36) | copy-start | bytes 1575940
  83.5 29.7 %all-to-all-start.1 = ((f32[1024,1,256]{2,1,0:T(1,128)}), f32[1024,1,256]{2,1,0:T(1,128)S(1)}, u32[]{:S(2)}, u32[]{:S(2)}) async-start(f32[1024,1,256]{2,1,0:T(1,128)} %copy.34), calls=%async_computation.1 | async-start | bytes 2097152 | tf_op jit(solution)/shard_map/all_to_all | solution.py:177
  89.2 24.1 %copy-start.14 = (f32[256]{0:T(256)}, f32[256]{0:T(256)S(1)}, u32[]{:S(2)}) copy-start(f32[256]{0:T(256)S(1)} %fusion.205) | copy-start | bytes 3076
  115.9 4.8 %collective-permute-start = (f32[1,16,256]{2,1,0:T(8,128)S(1)}, f32[1,16,256]{2,1,0:T(8,128)S(1)}, u32[]{:S(2)}, u32[]{:S(2)}) collective-permute-start(f32[1,16,256]{2,1,0:T(8,128)S(1)} %get-tuple-element.60), channel_id=1, source_target_pairs={{1,0},{2,1},{3,2},{4,3},{5,4},{6,5},{7,6},{8,7},{9,8},{10,9},{11,1... | collective-permute-start | bytes 49160 | tf_op jit(solution)/shard_map/ppermute | solution.py:37
  118.5 6.0 %collective-permute-start.1 = (f32[1,16,256]{2,1,0:T(8,128)S(1)}, f32[1,16,256]{2,1,0:T(8,128)S(1)}, u32[]{:S(2)}, u32[]{:S(2)}) collective-permute-start(f32[1,16,256]{2,1,0:T(8,128)S(1)} %get-tuple-element.61), channel_id=1, source_target_pairs={{0,1},{1,2},{2,3},{3,4},{4,5},{5,6},{6,7},{7,8},{8,9},{9,10},{10,1... | collective-permute-start | bytes 49160 | tf_op jit(solution)/shard_map/ppermute | solution.py:36
  125.7 5.2 %collective-permute-start.2 = (f32[1,16,256]{2,1,0:T(8,128)S(1)}, f32[1,16,256]{2,1,0:T(8,128)S(1)}, u32[]{:S(2)}, u32[]{:S(2)}) collective-permute-start(f32[1,16,256]{2,1,0:T(8,128)S(1)} %get-tuple-element.58), channel_id=1, source_target_pairs={{1,0},{2,1},{3,2},{4,3},{5,4},{6,5},{7,6},{8,7},{9,8},{10,9},{11,1... | collective-permute-start | bytes 49160 | tf_op jit(solution)/shard_map/ppermute | solution.py:37
  127.7 6.0 %collective-permute-start.3 = (f32[1,16,256]{2,1,0:T(8,128)S(1)}, f32[1,16,256]{2,1,0:T(8,128)S(1)}, u32[]{:S(2)}, u32[]{:S(2)}) collective-permute-start(f32[1,16,256]{2,1,0:T(8,128)S(1)} %get-tuple-element.59), channel_id=1, source_target_pairs={{0,1},{1,2},{2,3},{3,4},{4,5},{5,6},{6,7},{7,8},{8,9},{9,10},{10,1... | collective-permute-start | bytes 49160 | tf_op jit(solution)/shard_map/ppermute | solution.py:36
  137.1 4.4 %collective-permute-start.4 = (f32[1,16,256]{2,1,0:T(8,128)}, f32[1,16,256]{2,1,0:T(8,128)S(1)}, u32[]{:S(2)}, u32[]{:S(2)}) collective-permute-start(f32[1,16,256]{2,1,0:T(8,128)} %get-tuple-element.56), channel_id=1, source_target_pairs={{1,0},{2,1},{3,2},{4,3},{5,4},{6,5},{7,6},{8,7},{9,8},{10,9},{11,1... | collective-permute-start | bytes 49160 | tf_op jit(solution)/shard_map/ppermute | solution.py:37
  139.0 6.0 %collective-permute-start.5 = (f32[1,16,256]{2,1,0:T(8,128)S(1)}, f32[1,16,256]{2,1,0:T(8,128)S(1)}, u32[]{:S(2)}, u32[]{:S(2)}) collective-permute-start(f32[1,16,256]{2,1,0:T(8,128)S(1)} %get-tuple-element.57), channel_id=1, source_target_pairs={{0,1},{1,2},{2,3},{3,4},{4,5},{5,6},{6,7},{7,8},{8,9},{9,10},{10,1... | collective-permute-start | bytes 49160 | tf_op jit(solution)/shard_map/ppermute | solution.py:36
  151.1 7.9 %copy-start.4 = (f32[64,16,256]{2,1,0:T(8,128)}, f32[64,16,256]{2,1,0:T(8,128)S(1)}, u32[]{:S(2)}) copy-start(f32[64,16,256]{2,1,0:T(8,128)S(1)} %get-tuple-element.15) | copy-start | bytes 3145732
  151.1 5.1 %collective-permute-start.6 = (f32[1,16,256]{2,1,0:T(8,128)S(1)}, f32[1,16,256]{2,1,0:T(8,128)S(1)}, u32[]{:S(2)}, u32[]{:S(2)}) collective-permute-start(f32[1,16,256]{2,1,0:T(8,128)S(1)} %get-tuple-element.52), channel_id=1, source_target_pairs={{1,0},{2,1},{3,2},{4,3},{5,4},{6,5},{7,6},{8,7},{9,8},{10,9},{11,1... | collective-permute-start | bytes 49160 | tf_op jit(solution)/shard_map/ppermute | solution.py:37
  153.0 6.0 %collective-permute-start.7 = (f32[1,16,256]{2,1,0:T(8,128)S(1)}, f32[1,16,256]{2,1,0:T(8,128)S(1)}, u32[]{:S(2)}, u32[]{:S(2)}) collective-permute-start(f32[1,16,256]{2,1,0:T(8,128)S(1)} %get-tuple-element.53), channel_id=1, source_target_pairs={{0,1},{1,2},{2,3},{3,4},{4,5},{5,6},{6,7},{7,8},{8,9},{9,10},{10,1... | collective-permute-start | bytes 49160 | tf_op jit(solution)/shard_map/ppermute | solution.py:36
  162.9 3.7 %collective-permute-start.8 = (f32[64,1,256]{2,1,0:T(1,128)S(1)}, f32[64,1,256]{2,1,0:T(1,128)S(1)}, u32[]{:S(2)}, u32[]{:S(2)}) collective-permute-start(f32[64,1,256]{2,1,0:T(1,128)S(1)} %get-tuple-element.51), channel_id=1, source_target_pairs={{0,1},{1,0},{2,3},{3,2},{4,5},{5,4},{6,7},{7,6},{8,9},{9,8},{10,11... | collective-permute-start | bytes 196616 | tf_op jit(solution)/shard_map/ppermute | solution.py:167
  162.9 5.5 %collective-permute-start.9 = (f32[64,1,256]{2,1,0:T(1,128)S(1)}, f32[64,1,256]{2,1,0:T(1,128)S(1)}, u32[]{:S(2)}, u32[]{:S(2)}) collective-permute-start(f32[64,1,256]{2,1,0:T(1,128)S(1)} %get-tuple-element.50), channel_id=1, source_target_pairs={{0,2},{1,3},{2,0},{3,1},{4,6},{5,7},{6,4},{7,5},{8,10},{9,11},{10,... | collective-permute-start | bytes 196616 | tf_op jit(solution)/shard_map/ppermute | solution.py:167
  165.0 4.6 %collective-permute-start.10 = (f32[64,1,256]{2,1,0:T(1,128)S(1)}, f32[64,1,256]{2,1,0:T(1,128)S(1)}, u32[]{:S(2)}, u32[]{:S(2)}) collective-permute-start(f32[64,1,256]{2,1,0:T(1,128)S(1)} %get-tuple-element.49), channel_id=1, source_target_pairs={{0,3},{1,2},{2,1},{3,0},{4,7},{5,6},{6,5},{7,4},{8,11},{9,10},{10,... | collective-permute-start | bytes 196616 | tf_op jit(solution)/shard_map/ppermute | solution.py:167
  165.0 6.7 %collective-permute-start.11 = (f32[64,1,256]{2,1,0:T(1,128)S(1)}, f32[64,1,256]{2,1,0:T(1,128)S(1)}, u32[]{:S(2)}, u32[]{:S(2)}) collective-permute-start(f32[64,1,256]{2,1,0:T(1,128)S(1)} %get-tuple-element.48), channel_id=1, source_target_pairs={{0,4},{1,5},{2,6},{3,7},{4,0},{5,1},{6,2},{7,3},{8,12},{9,13},{10,... | collective-permute-start | bytes 196616 | tf_op jit(solution)/shard_map/ppermute | solution.py:167
  165.0 7.2 %collective-permute-start.12 = (f32[64,1,256]{2,1,0:T(1,128)S(1)}, f32[64,1,256]{2,1,0:T(1,128)S(1)}, u32[]{:S(2)}, u32[]{:S(2)}) collective-permute-start(f32[64,1,256]{2,1,0:T(1,128)S(1)} %get-tuple-element.47), channel_id=1, source_target_pairs={{0,5},{1,4},{2,7},{3,6},{4,1},{5,0},{6,3},{7,2},{8,13},{9,12},{10,... | collective-permute-start | bytes 196616 | tf_op jit(solution)/shard_map/ppermute | solution.py:167
  166.6 9.2 %collective-permute-start.13 = (f32[64,1,256]{2,1,0:T(1,128)S(1)}, f32[64,1,256]{2,1,0:T(1,128)S(1)}, u32[]{:S(2)}, u32[]{:S(2)}) collective-permute-start(f32[64,1,256]{2,1,0:T(1,128)S(1)} %get-tuple-element.46), channel_id=1, source_target_pairs={{0,6},{1,7},{2,4},{3,5},{4,2},{5,3},{6,0},{7,1},{8,14},{9,15},{10,... | collective-permute-start | bytes 196616 | tf_op jit(solution)/shard_map/ppermute | solution.py:167
  168.4 7.8 %collective-permute-start.14 = (f32[64,1,256]{2,1,0:T(1,128)S(1)}, f32[64,1,256]{2,1,0:T(1,128)S(1)}, u32[]{:S(2)}, u32[]{:S(2)}) collective-permute-start(f32[64,1,256]{2,1,0:T(1,128)S(1)} %get-tuple-element.45), channel_id=1, source_target_pairs={{0,7},{1,6},{2,5},{3,4},{4,3},{5,2},{6,1},{7,0},{8,15},{9,14},{10,... | collective-permute-start | bytes 196616 | tf_op jit(solution)/shard_map/ppermute | solution.py:167
  169.7 10.1 %collective-permute-start.15 = (f32[64,1,256]{2,1,0:T(1,128)S(1)}, f32[64,1,256]{2,1,0:T(1,128)S(1)}, u32[]{:S(2)}, u32[]{:S(2)}) collective-permute-start(f32[64,1,256]{2,1,0:T(1,128)S(1)} %get-tuple-element.44), channel_id=1, source_target_pairs={{0,8},{1,9},{2,10},{3,11},{4,12},{5,13},{6,14},{7,15},{8,0},{9,1},... | collective-permute-start | bytes 196616 | tf_op jit(solution)/shard_map/ppermute | solution.py:167
  171.8 11.6 %collective-permute-start.16 = (f32[64,1,256]{2,1,0:T(1,128)S(1)}, f32[64,1,256]{2,1,0:T(1,128)S(1)}, u32[]{:S(2)}, u32[]{:S(2)}) collective-permute-start(f32[64,1,256]{2,1,0:T(1,128)S(1)} %get-tuple-element.43), channel_id=1, source_target_pairs={{0,9},{1,8},{2,11},{3,10},{4,13},{5,12},{6,15},{7,14},{8,1},{9,0},... | collective-permute-start | bytes 196616 | tf_op jit(solution)/shard_map/ppermute | solution.py:167
  172.2 12.7 %collective-permute-start.17 = (f32[64,1,256]{2,1,0:T(1,128)S(1)}, f32[64,1,256]{2,1,0:T(1,128)S(1)}, u32[]{:S(2)}, u32[]{:S(2)}) collective-permute-start(f32[64,1,256]{2,1,0:T(1,128)S(1)} %get-tuple-element.42), channel_id=1, source_target_pairs={{0,10},{1,11},{2,8},{3,9},{4,14},{5,15},{6,12},{7,13},{8,2},{9,3},... | collective-permute-start | bytes 196616 | tf_op jit(solution)/shard_map/ppermute | solution.py:167
  175.8 11.1 %collective-permute-start.18 = (f32[64,1,256]{2,1,0:T(1,128)S(1)}, f32[64,1,256]{2,1,0:T(1,128)S(1)}, u32[]{:S(2)}, u32[]{:S(2)}) collective-permute-start(f32[64,1,256]{2,1,0:T(1,128)S(1)} %get-tuple-element.41), channel_id=1, source_target_pairs={{0,11},{1,10},{2,9},{3,8},{4,15},{5,14},{6,13},{7,12},{8,3},{9,2},... | collective-permute-start | bytes 196616 | tf_op jit(solution)/shard_map/ppermute | solution.py:167
  176.2 14.8 %collective-permute-start.19 = (f32[64,1,256]{2,1,0:T(1,128)S(1)}, f32[64,1,256]{2,1,0:T(1,128)S(1)}, u32[]{:S(2)}, u32[]{:S(2)}) collective-permute-start(f32[64,1,256]{2,1,0:T(1,128)S(1)} %get-tuple-element.40), channel_id=1, source_target_pairs={{0,12},{1,13},{2,14},{3,15},{4,8},{5,9},{6,10},{7,11},{8,4},{9,5},... | collective-permute-start | bytes 196616 | tf_op jit(solution)/shard_map/ppermute | solution.py:167
  179.7 12.7 %collective-permute-start.20 = (f32[64,1,256]{2,1,0:T(1,128)S(1)}, f32[64,1,256]{2,1,0:T(1,128)S(1)}, u32[]{:S(2)}, u32[]{:S(2)}) collective-permute-start(f32[64,1,256]{2,1,0:T(1,128)S(1)} %get-tuple-element.39), channel_id=1, source_target_pairs={{0,13},{1,12},{2,15},{3,14},{4,9},{5,8},{6,11},{7,10},{8,5},{9,4},... | collective-permute-start | bytes 196616 | tf_op jit(solution)/shard_map/ppermute | solution.py:167
  183.4 11.9 %collective-permute-start.21 = (f32[64,1,256]{2,1,0:T(1,128)S(1)}, f32[64,1,256]{2,1,0:T(1,128)S(1)}, u32[]{:S(2)}, u32[]{:S(2)}) collective-permute-start(f32[64,1,256]{2,1,0:T(1,128)S(1)} %get-tuple-element.38), channel_id=1, source_target_pairs={{0,14},{1,15},{2,12},{3,13},{4,10},{5,11},{6,8},{7,9},{8,6},{9,7},... | collective-permute-start | bytes 196616 | tf_op jit(solution)/shard_map/ppermute | solution.py:167
  184.9 11.8 %collective-permute-start.22 = (f32[64,1,256]{2,1,0:T(1,128)S(1)}, f32[64,1,256]{2,1,0:T(1,128)S(1)}, u32[]{:S(2)}, u32[]{:S(2)}) collective-permute-start(f32[64,1,256]{2,1,0:T(1,128)S(1)} %get-tuple-element.37), channel_id=1, source_target_pairs={{0,15},{1,14},{2,13},{3,12},{4,11},{5,10},{6,9},{7,8},{8,7},{9,6},... | collective-permute-start | bytes 196616 | tf_op jit(solution)/shard_map/ppermute | solution.py:167
  198.4 12.3 %copy-start.8 = (f32[16,64,256]{2,1,0:T(8,128)S(1)}, f32[16,64,256]{2,1,0:T(8,128)}, u32[]{:S(2)}) copy-start(f32[16,64,256]{2,1,0:T(8,128)} %gather_fusion) | copy-start | bytes 3145732
  198.4 12.4 %copy-start.13 = (f32[513,127]{0,1:T(8,128)S(1)}, f32[513,127]{0,1:T(8,128)}, u32[]{:S(2)}) copy-start(f32[513,127]{0,1:T(8,128)} %copy-done.12) | copy-start | bytes 781816
  198.4 12.4 %copy-start.20 = (f32[513,256]{0,1:T(8,128)S(1)}, f32[513,256]{0,1:T(8,128)}, u32[]{:S(2)}) copy-start(f32[513,256]{0,1:T(8,128)} %copy-done.19) | copy-start | bytes 1575940
  210.7 10.8 %copy-start.17 = (f32[513]{0:T(1024)S(1)}, f32[513]{0:T(1024)}, u32[]{:S(2)}) copy-start(f32[513]{0:T(1024)} %copy-done.16) | copy-start | bytes 6160
  276.4 11.8 %copy-start.5 = (f32[64,16,256]{2,1,0:T(8,128)S(1)}, f32[64,16,256]{2,1,0:T(8,128)}, u32[]{:S(2)}) copy-start(f32[64,16,256]{2,1,0:T(8,128)} %copy-done.4) | copy-start | bytes 3145732
  276.4 11.8 %copy-start.7 = (f32[64,16,256]{2,1,0:T(8,128)S(1)}, f32[64,16,256]{2,1,0:T(8,128)}, u32[]{:S(2)}) copy-start(f32[64,16,256]{2,1,0:T(8,128)} %copy-done.6) | copy-start | bytes 3145732
  279.0 5.2 %collective-permute-start.23 = (f32[1,16,256]{2,1,0:T(8,128)S(1)}, f32[1,16,256]{2,1,0:T(8,128)S(1)}, u32[]{:S(2)}, u32[]{:S(2)}) collective-permute-start(f32[1,16,256]{2,1,0:T(8,128)S(1)} %get-tuple-element.35), channel_id=1, source_target_pairs={{1,0},{2,1},{3,2},{4,3},{5,4},{6,5},{7,6},{8,7},{9,8},{10,9},{11,1... | collective-permute-start | bytes 49160 | tf_op jit(solution)/shard_map/ppermute | solution.py:37
  282.3 6.0 %collective-permute-start.24 = (f32[1,16,256]{2,1,0:T(8,128)S(1)}, f32[1,16,256]{2,1,0:T(8,128)S(1)}, u32[]{:S(2)}, u32[]{:S(2)}) collective-permute-start(f32[1,16,256]{2,1,0:T(8,128)S(1)} %get-tuple-element.36), channel_id=1, source_target_pairs={{0,1},{1,2},{2,3},{3,4},{4,5},{5,6},{6,7},{7,8},{8,9},{9,10},{10,1... | collective-permute-start | bytes 49160 | tf_op jit(solution)/shard_map/ppermute | solution.py:36
  289.8 5.0 %collective-permute-start.25 = (f32[1,16,256]{2,1,0:T(8,128)S(1)}, f32[1,16,256]{2,1,0:T(8,128)S(1)}, u32[]{:S(2)}, u32[]{:S(2)}) collective-permute-start(f32[1,16,256]{2,1,0:T(8,128)S(1)} %get-tuple-element.31), channel_id=1, source_target_pairs={{1,0},{2,1},{3,2},{4,3},{5,4},{6,5},{7,6},{8,7},{9,8},{10,9},{11,1... | collective-permute-start | bytes 49160 | tf_op jit(solution)/shard_map/ppermute | solution.py:37
  291.7 6.0 %collective-permute-start.26 = (f32[1,16,256]{2,1,0:T(8,128)S(1)}, f32[1,16,256]{2,1,0:T(8,128)S(1)}, u32[]{:S(2)}, u32[]{:S(2)}) collective-permute-start(f32[1,16,256]{2,1,0:T(8,128)S(1)} %get-tuple-element.32), channel_id=1, source_target_pairs={{0,1},{1,2},{2,3},{3,4},{4,5},{5,6},{6,7},{7,8},{8,9},{9,10},{10,1... | collective-permute-start | bytes 49160 | tf_op jit(solution)/shard_map/ppermute | solution.py:36
  298.6 4.3 %collective-permute-start.27 = (f32[1,16,256]{2,1,0:T(8,128)S(1)}, f32[1,16,256]{2,1,0:T(8,128)S(1)}, u32[]{:S(2)}, u32[]{:S(2)}) collective-permute-start(f32[1,16,256]{2,1,0:T(8,128)S(1)} %get-tuple-element.29), channel_id=1, source_target_pairs={{1,0},{2,1},{3,2},{4,3},{5,4},{6,5},{7,6},{8,7},{9,8},{10,9},{11,1... | collective-permute-start | bytes 49160 | tf_op jit(solution)/shard_map/ppermute | solution.py:37
  300.6 6.0 %collective-permute-start.28 = (f32[1,16,256]{2,1,0:T(8,128)S(1)}, f32[1,16,256]{2,1,0:T(8,128)S(1)}, u32[]{:S(2)}, u32[]{:S(2)}) collective-permute-start(f32[1,16,256]{2,1,0:T(8,128)S(1)} %get-tuple-element.30), channel_id=1, source_target_pairs={{0,1},{1,2},{2,3},{3,4},{4,5},{5,6},{6,7},{7,8},{8,9},{9,10},{10,1... | collective-permute-start | bytes 49160 | tf_op jit(solution)/shard_map/ppermute | solution.py:36
  308.1 4.8 %collective-permute-start.29 = (f32[1,16,256]{2,1,0:T(8,128)S(1)}, f32[1,16,256]{2,1,0:T(8,128)S(1)}, u32[]{:S(2)}, u32[]{:S(2)}) collective-permute-start(f32[1,16,256]{2,1,0:T(8,128)S(1)} %get-tuple-element.25), channel_id=1, source_target_pairs={{1,0},{2,1},{3,2},{4,3},{5,4},{6,5},{7,6},{8,7},{9,8},{10,9},{11,1... | collective-permute-start | bytes 49160 | tf_op jit(solution)/shard_map/ppermute | solution.py:37
  310.0 6.0 %collective-permute-start.30 = (f32[1,16,256]{2,1,0:T(8,128)S(1)}, f32[1,16,256]{2,1,0:T(8,128)S(1)}, u32[]{:S(2)}, u32[]{:S(2)}) collective-permute-start(f32[1,16,256]{2,1,0:T(8,128)S(1)} %get-tuple-element.26), channel_id=1, source_target_pairs={{0,1},{1,2},{2,3},{3,4},{4,5},{5,6},{6,7},{7,8},{8,9},{9,10},{10,1... | collective-permute-start | bytes 49160 | tf_op jit(solution)/shard_map/ppermute | solution.py:36
  (7 other events, 18.0 us)
